TPU v7x, 32 devices: a whole 2x2x4 slice. The times are simulated.
32 devices in a mesh: dp: 2 (over y), pipe: 4 (over x, core), seq: 4 (over z).
Axes of the slice: x: 2, y: 2, z: 4, core: 2. Of those that a mesh axis runs over, the one named last changes fastest.
Arguments:
- query_states: bfloat16 [8, 512, 8192], P(('dp', 'pipe'), 'seq'), parts along dimension 0, may hold values from -15 to 15
- projected_keys: bfloat16 [8, 512, 1024], P(('dp', 'pipe'), 'seq'), parts along dimension 0, may hold values from -8 to 8
- projected_values: bfloat16 [8, 512, 1024], P(('dp', 'pipe'), 'seq'), parts along dimension 0, may hold values from -6 to 6
- positions: int32 [8, 512], P(('dp', 'pipe'), 'seq'), parts along dimension 0, may hold values from 0 to 1023, as said below
- segments: int32 [8, 512], P(('dp', 'pipe'), 'seq'), parts along dimension 0, may hold values from 0 to 3, as said below
Outputs:
- handed: bfloat16 [8, 512, 8192], P(('dp', 'pipe'), 'seq'), parts along dimension 0
There are 2 independent parts, one for each index of `dp`. A program takes and returns all parts, laid end to end along the dimension named above; each array names one. Nothing has to cross between parts.
Inputs may be any that keep to these rules, and one draw needn't show every extreme that they name: `segments`: within each micro-batch ids never fall along the sequence, start at 0, every id occurs, and every document holds 4 or more tokens. `positions`: within a document a position is one more than the previous token's; the first document of each micro-batch starts at 0, and the last token of each micro-batch has position 1023.
All inputs are finite; a program needn't handle non-finite values.
Results may differ from a plain program's by a relative error of at most 0.0014.
The roundings to bfloat16 on the way count: a program that leaves them out, or rounds other values in their place, can miss the bound.
Values may be sent and summed in bfloat16 or wider, within the bound.
No kernel may reach another device: no remote copies, remote signals or barrier semaphores. Data moves between devices by JAX's collectives and lax.ppermute only.
A program may use at most 64 MiB of HBM per device.

v0:
```python
import math
import jax
import jax.numpy as jnp
from jax import lax
from jax.sharding import PartitionSpec as P

QUERY_HEADS = 64
KEY_VALUE_HEADS = 8
HEAD_SIZE = 128
rope_theta = 1000000.0
yarn_factor = 4.0
trained_length = 32768.0
fast_beta = 32.0
slow_beta = 1.0
masked_score = -1e30


def passed_along(block, axis, distance):
    devices = range(lax.axis_size(axis))
    route = [((i - distance) % len(devices), i) for i in devices]
    return lax.ppermute(block, axis, route)


def yarn_tables(positions, head_dim):
    half_dim = head_dim // 2
    pair_index = jnp.arange(half_dim, dtype=jnp.float32)
    base_freq = 1.0 / rope_theta ** (2.0 * pair_index / head_dim)
    lower = math.floor(
        head_dim
        * math.log(trained_length / (fast_beta * 2.0 * math.pi))
        / (2.0 * math.log(rope_theta))
    )
    upper = math.ceil(
        head_dim
        * math.log(trained_length / (slow_beta * 2.0 * math.pi))
        / (2.0 * math.log(rope_theta))
    )
    lower = max(lower, 0)
    upper = min(upper, head_dim - 1)
    upper = max(upper, lower + 1)
    ramp_value = jnp.clip((pair_index - lower) / (upper - lower), 0.0, 1.0)
    keep_share = 1.0 - ramp_value
    inv_freq = base_freq / yarn_factor * (1.0 - keep_share) + base_freq * keep_share
    attn_gain = 0.1 * math.log(yarn_factor) + 1.0
    angles = positions.astype(jnp.float32)[..., None] * inv_freq
    return (jnp.cos(angles) * attn_gain, jnp.sin(angles) * attn_gain)


def apply_rotation(states, cosine_table, sine_table):
    half_dim = states.shape[-1] // 2
    first_half = states[..., :half_dim]
    second_half = states[..., half_dim:]
    return jnp.concatenate(
        [
            first_half * cosine_table - second_half * sine_table,
            second_half * cosine_table + first_half * sine_table,
        ],
        axis=-1,
    )


def empty_running(query_rows, kv_count, group_count):
    return (
        jnp.full((query_rows, kv_count, group_count), masked_score, jnp.float32),
        jnp.zeros((query_rows, kv_count, group_count), jnp.float32),
        jnp.zeros((query_rows, kv_count, group_count, HEAD_SIZE), jnp.float32),
    )


def online_update(running, query_block, key_block, value_block, visible):
    best, denom, accum = running
    scores = jnp.einsum(
        "qkgd,nkd->qkgn", query_block, key_block, preferred_element_type=jnp.float32
    ) / math.sqrt(HEAD_SIZE)
    shown = visible[:, None, None, :]
    scores = jnp.where(shown, scores, masked_score)
    best_next = jnp.maximum(best, jnp.max(scores, axis=-1))
    weights = jnp.where(shown, jnp.exp(scores - best_next[..., None]), 0.0)
    rescale = jnp.exp(best - best_next)
    denom = denom * rescale + jnp.sum(weights, axis=-1)
    accum = accum * rescale[..., None] + jnp.einsum(
        "qkgn,nkd->qkgd",
        weights.astype(jnp.bfloat16),
        value_block,
        preferred_element_type=jnp.float32,
    )
    return (best_next, denom, accum)


def finish_running(running):
    best, denom, accum = running
    result = accum / denom[..., None]
    return result.reshape(result.shape[0], -1).astype(jnp.bfloat16)


def attend_local(grouped_queries, key_heads, value_head_rows, segment_ids):
    sequence_total = grouped_queries.shape[0]
    kv_count = grouped_queries.shape[1]
    group_count = grouped_queries.shape[2]
    block = min(512, sequence_total)
    block_count = sequence_total // block

    def one_block(block_index, finished):
        first_row = block_index * block
        query_block = lax.dynamic_slice_in_dim(grouped_queries, first_row, block, 0)
        query_segs = lax.dynamic_slice_in_dim(segment_ids, first_row, block, 0)
        query_ids = first_row + jnp.arange(block, dtype=jnp.int32)

        def key_step(key_index, running):
            first_key = key_index * block
            key_block = lax.dynamic_slice_in_dim(key_heads, first_key, block, 0)
            value_block = lax.dynamic_slice_in_dim(value_head_rows, first_key, block, 0)
            key_segs = lax.dynamic_slice_in_dim(segment_ids, first_key, block, 0)
            key_ids = first_key + jnp.arange(block, dtype=jnp.int32)
            visible = (key_ids[None, :] <= query_ids[:, None]) & (
                key_segs[None, :] == query_segs[:, None]
            )
            return online_update(running, query_block, key_block, value_block, visible)

        running = lax.fori_loop(
            0, block_index + 1, key_step, empty_running(block, kv_count, group_count)
        )
        return lax.dynamic_update_slice_in_dim(finished, finish_running(running), first_row, 0)

    finished = jnp.zeros((sequence_total, kv_count * group_count * HEAD_SIZE), jnp.bfloat16)
    return lax.fori_loop(0, block_count, one_block, finished)


def on_device(query_states, projected_keys, projected_values, positions, segments):
    token_rows = query_states.shape[1]
    cosine_table, sine_table = yarn_tables(positions[0], HEAD_SIZE)
    cosine_table = cosine_table[:, None, :]
    sine_table = sine_table[:, None, :]
    rotated_queries = apply_rotation(
        query_states[0].astype(jnp.float32).reshape(token_rows, QUERY_HEADS, HEAD_SIZE),
        cosine_table,
        sine_table,
    ).astype(jnp.bfloat16)
    rotated_keys = apply_rotation(
        projected_keys[0].astype(jnp.float32).reshape(token_rows, KEY_VALUE_HEADS, HEAD_SIZE),
        cosine_table,
        sine_table,
    ).astype(jnp.bfloat16)
    value_head_rows = projected_values[0].reshape(token_rows, KEY_VALUE_HEADS, HEAD_SIZE)
    segment_ids = segments[0]
    row_width = lax.axis_size("seq")
    per_device = QUERY_HEADS // row_width
    key_value_local = max(1, KEY_VALUE_HEADS // row_width)
    repeat_count = max(1, row_width // KEY_VALUE_HEADS)
    query_send = rotated_queries.reshape(token_rows, row_width, per_device * HEAD_SIZE)
    key_send = jnp.broadcast_to(
        rotated_keys.reshape(
            token_rows, KEY_VALUE_HEADS // key_value_local, 1, key_value_local * HEAD_SIZE
        ),
        (token_rows, KEY_VALUE_HEADS // key_value_local, repeat_count, key_value_local * HEAD_SIZE),
    ).reshape(token_rows, row_width, key_value_local * HEAD_SIZE)
    value_send = jnp.broadcast_to(
        value_head_rows.reshape(
            token_rows, KEY_VALUE_HEADS // key_value_local, 1, key_value_local * HEAD_SIZE
        ),
        (token_rows, KEY_VALUE_HEADS // key_value_local, repeat_count, key_value_local * HEAD_SIZE),
    ).reshape(token_rows, row_width, key_value_local * HEAD_SIZE)
    segment_send = jnp.broadcast_to(
        segment_ids.astype(jnp.bfloat16)[:, None, None], (token_rows, row_width, 1)
    )
    query_all, key_all, value_all, segment_all = (
        lax.all_to_all(query_send, "seq", split_axis=1, concat_axis=0, tiled=True),
        lax.all_to_all(key_send, "seq", split_axis=1, concat_axis=0, tiled=True),
        lax.all_to_all(value_send, "seq", split_axis=1, concat_axis=0, tiled=True),
        lax.all_to_all(segment_send, "seq", split_axis=1, concat_axis=0, tiled=True),
    )
    sequence_total = token_rows * row_width
    heads_out = attend_local(
        query_all.reshape(
            sequence_total, key_value_local, per_device // key_value_local, HEAD_SIZE
        ),
        key_all.reshape(sequence_total, key_value_local, HEAD_SIZE),
        value_all.reshape(sequence_total, key_value_local, HEAD_SIZE),
        segment_all.reshape(sequence_total).astype(jnp.int32),
    )
    rows_out = lax.all_to_all(
        heads_out.reshape(sequence_total, 1, per_device * HEAD_SIZE),
        "seq",
        split_axis=0,
        concat_axis=1,
        tiled=True,
    )
    rows_out = rows_out.reshape(token_rows, QUERY_HEADS * HEAD_SIZE)
    rows_out = passed_along(rows_out, "pipe", 1)
    return rows_out[None]


def solution(mesh):
    placed = (
        P(("dp", "pipe"), "seq", None),
        P(("dp", "pipe"), "seq", None),
        P(("dp", "pipe"), "seq", None),
        P(("dp", "pipe"), "seq"),
        P(("dp", "pipe"), "seq"),
    )
    return jax.shard_map(
        on_device,
        mesh=mesh,
        in_specs=placed,
        out_specs=P(("dp", "pipe"), "seq", None),
        check_vma=False,
    )
```

profile of v0, /device:TPU:0, one launch (start us, length us, event | category | flops | bytes accessed | tf_op | source)
XLA Modules:
  0.0 201.0 jit_solution(10546775687055647915)
XLA Ops:
  0.0 0.0 copy-start
  0.0 0.8 convert_bitcast_fusion.1
  0.8 0.6 broadcast_in_dim.51
  1.4 6.3 %all-to-all-start = ((bf16[128,4,1]{0,2,1:T(2,128)(2,1)}), bf16[128,4,1]{0,2,1:T(2,128)(2,1)S(1)}, u32[]{:S(2)}, u32[]{:S(2)}) async-start(bf16[128,4,1]{0,2,1:T(2,128)(2,1)} %broadcast_in_dim.51), calls=%async_computation | async-start | bytes 4096 | tf_op jit(solution)/shard_map/all_to_all | solution.py:170
  7.8 0.7 convert_bitcast_fusion
  8.4 1.1 copy.44
  9.5 0.0 copy-start.1
  9.5 0.2 fusion.15
  9.7 0.1 subtract_convert_fusion.1
  9.8 0.7 pad_maximum_fusion.1
  10.5 2.8 %all-to-all-done = bf16[128,4,1]{0,2,1:T(2,128)(2,1)S(1)} async-done(((bf16[128,4,1]{0,2,1:T(2,128)(2,1)}), bf16[128,4,1]{0,2,1:T(2,128)(2,1)S(1)}, u32[]{:S(2)}, u32[]{:S(2)}) %all-to-all-start) | async-done | bytes 1056 | tf_op jit(solution)/shard_map/all_to_all | solution.py:170
  13.3 3.4 %all-to-all-start.1 = ((bf16[128,4,256]{0,2,1:T(8,128)(2,1)}), bf16[128,4,256]{0,2,1:T(8,128)(2,1)S(1)}, u32[]{:S(2)}, u32[]{:S(2)}) async-start(bf16[128,4,256]{0,2,1:T(8,128)(2,1)} %bitcast.8), calls=%async_computation.1 | async-start | bytes 524288 | tf_op jit(solution)/shard_map/all_to_all | solution.py:168
  16.7 0.0 copy-done
  16.7 2.9 %copy.46 = f32[1,128,8192]{1,2,0:T(8,128)} copy(bf16[1,128,8192]{2,1,0:T(8,128)(2,1)S(1)} %copy-done) | data formatting | bytes 6291456 | tf_op jit(solution)/shard_map/convert_element_type | solution.py:135
  19.7 0.0 copy-done.1
  19.7 0.8 copy.50
  20.5 3.3 %all-to-all-done.1 = bf16[128,4,256]{0,2,1:T(8,128)(2,1)S(1)} async-done(((bf16[128,4,256]{0,2,1:T(8,128)(2,1)}), bf16[128,4,256]{0,2,1:T(8,128)(2,1)S(1)}, u32[]{:S(2)}, u32[]{:S(2)}) %all-to-all-start.1) | async-done | bytes 262176 | tf_op jit(solution)/shard_map/all_to_all | solution.py:168
  23.8 3.4 %all-to-all-start.3 = ((bf16[128,4,256]{0,2,1:T(8,128)(2,1)}), bf16[128,4,256]{0,2,1:T(8,128)(2,1)S(1)}, u32[]{:S(2)}, u32[]{:S(2)}) async-start(bf16[128,4,256]{0,2,1:T(8,128)(2,1)} %bitcast.17), calls=%async_computation.3 | async-start | bytes 524288 | tf_op jit(solution)/shard_map/all_to_all | solution.py:169
  27.2 2.8 %subtract_convert_fusion = (bf16[128,64,64]{0,2,1:T(8,128)(2,1)S(1)}, bf16[128,64,64]{0,2,1:T(8,128)(2,1)S(1)}) fusion(f32[128,64,128]{0,2,1:T(8,128)} %bitcast.64, f32[128,64]{0,1:T(8,128)S(1)} %get-tuple-element.110, f32[128,64]{0,1:T(8,128)S(1)} %get-tuple-element.109), kind=kLoop, calls=%fused_computation.14 | loop fusion | flops 4194304 | bytes 6356992 | tf_op jit(solution)/shard_map/convert.5
  30.0 1.5 pad_maximum_fusion
  31.6 2.4 %all-to-all-done.3 = bf16[128,4,256]{0,2,1:T(8,128)(2,1)S(1)} async-done(((bf16[128,4,256]{0,2,1:T(8,128)(2,1)}), bf16[128,4,256]{0,2,1:T(8,128)(2,1)S(1)}, u32[]{:S(2)}, u32[]{:S(2)}) %all-to-all-start.3) | async-done | bytes 262176 | tf_op jit(solution)/shard_map/all_to_all | solution.py:169
  33.9 3.6 %all-to-all-start.2 = ((bf16[128,4,2048]{0,2,1:T(8,128)(2,1)}), bf16[128,4,2048]{0,2,1:T(8,128)(2,1)S(1)}, u32[]{:S(2)}, u32[]{:S(2)}) async-start(bf16[128,4,2048]{0,2,1:T(8,128)(2,1)} %bitcast.13), calls=%async_computation.2 | async-start | bytes 4194304 | tf_op jit(solution)/shard_map/all_to_all | solution.py:167
  37.6 0.2 fusion.12
  37.8 0.1 copy.45
  37.9 0.1 reshape.183
  38.0 0.2 copy.51
  38.2 0.1 reshape.192
  38.3 43.6 %all-to-all-done.2 = bf16[128,4,2048]{0,2,1:T(8,128)(2,1)S(1)} async-done(((bf16[128,4,2048]{0,2,1:T(8,128)(2,1)}), bf16[128,4,2048]{0,2,1:T(8,128)(2,1)S(1)}, u32[]{:S(2)}, u32[]{:S(2)}) %all-to-all-start.2) | async-done | bytes 2097184 | tf_op jit(solution)/shard_map/all_to_all | solution.py:167
  82.0 2.6 %copy.47 = bf16[4,128,1,2048]{3,1,0,2:T(8,128)(2,1)} copy(bf16[4,128,1,2048]{1,3,0,2:T(8,128)(2,1)S(1)} %bitcast.67) | data formatting | bytes 4194304 | tf_op jit(solution)/shard_map/all_to_all | solution.py:167
  84.6 2.2 %copy.62 = bf16[64,8,16,128]{3,2,1,0:T(8,128)(2,1)S(1)} copy(bf16[64,8,16,128]{3,1,2,0:T(8,128)(2,1)} %bitcast.68) | data formatting | bytes 4194304
  86.8 3.8 %fusion = (f32[512,2,8]{0,2,1:T(8,128)S(1)}, f32[2,512,512,8]{2,1,3,0:T(8,128)S(1)}) fusion(pred[512,512]{0,1:T(8,128)(4,1)S(1)} %fusion.12, bf16[512,2,8,128]{3,2,1,0:T(8,128)(2,1)S(1)} %bitcast.65, bf16[512,2,128,1]{2,1,0,3:T(2,128)(2,1)S(1)} %bitcast.73), kind=kOutput, calls=%fused_computation.2 | convolution fusion | flops 1086316544 | bytes 19431424 | tf_op jit(solution)/shard_map/while/body/eval_jaxpr/while/body/qkgd,nkd->qkgn/dot_general | solution.py:72
  90.6 4.0 %fusion.1 = f32[512,2,8]{0,2,1:T(8,128)S(1)} fusion(f32[2,512,512,8]{2,1,3,0:T(8,128)S(1)} %get-tuple-element.112, f32[512,2,8]{0,2,1:T(8,128)S(1)} %broadcast_maximum_fusion, pred[512,512]{0,1:T(8,128)(4,1)S(1)} %fusion.12), kind=kLoop, calls=%fused_computation.3 | loop fusion | flops 20963328 | bytes 17104896 | tf_op jit(solution)/shard_map/while/body/eval_jaxpr/while/body/reduce_sum | solution.py:80
  94.6 6.0 %fusion.7 = bf16[512,2,8,128]{0,3,2,1:T(8,128)(2,1)} fusion(f32[2,512,512,8]{2,1,3,0:T(8,128)S(1)} %get-tuple-element.112, f32[512,2,8]{0,2,1:T(8,128)S(1)} %broadcast_maximum_fusion, pred[512,512]{0,1:T(8,128)(4,1)S(1)} %fusion.12, f32[512,2,8]{0,2,1:T(8,128)S(1)} %get-tuple-element.108, f32[512,2,8]{0,2,1:T(8,128)S(1)} %get-tuple-element.107, ...), kind=kOutput, calls=%fused_computation.9 | convolution fusion | flops 1097859072 | bytes 19496960 | tf_op jit(solution)/shard_map/while/body/eval_jaxpr/while/body/qkgn,nkd->qkgd/dot_general | solution.py:81
  100.7 0.5 broadcast.185
  101.2 3.8 %reduce = bf16[512,2048]{0,1:T(8,128)(2,1)S(1)} reduce(bf16[512,1,2048]{0,2,1:T(8,128)(2,1)} %bitcast.69, bf16[]{:T(256)} %broadcast.185), dimensions={1}, to_apply=%copy.53.reduce_sub_computation | reduce | bytes 4194306 | tf_op jit(solution)/shard_map/while/body/eval_jaxpr/convert_element_type | solution.py:93
  105.0 2.4 %copy.71 = bf16[512,2048]{1,0:T(8,128)(2,1)} copy(bf16[512,2048]{0,1:T(8,128)(2,1)S(1)} %reduce) | data formatting | bytes 4194304
  107.4 4.5 %reshape.194 = bf16[4,2,131072]{2,1,0:T(2,128)(2,1)} reshape(bf16[512,2048]{1,0:T(8,128)(2,1)} %copy.71) | data formatting | bytes 4194304
  111.9 51.3 %all_to_all.69 = bf16[4,2,131072]{2,1,0:T(2,128)(2,1)S(1)} all-to-all(bf16[4,2,131072]{2,1,0:T(2,128)(2,1)} %reshape.194), channel_id=1, replica_groups=mesh['dp'=2,'pipe'=4,'seq'=4] {'seq'}, dimensions={0} | all-to-all | bytes 4194304 | tf_op jit(solution)/shard_map/all_to_all | solution.py:181
  163.2 3.4 %reshape.195 = bf16[512,1,2048]{2,1,0:T(2,128)(2,1)} reshape(bf16[4,2,131072]{2,1,0:T(2,128)(2,1)S(1)} %all_to_all.69) | data formatting | bytes 4194304
  166.5 3.5 %copy.61 = bf16[512,1,2048]{2,0,1:T(8,128)(2,1)S(1)} copy(bf16[512,1,2048]{2,1,0:T(2,128)(2,1)} %reshape.195) | data formatting | bytes 4194304
  170.0 2.5 %copy.54 = bf16[128,4,1,2048]{0,3,1,2:T(8,128)(2,1)} copy(bf16[128,4,1,2048]{3,0,1,2:T(8,128)(2,1)S(1)} %bitcast.66) | data formatting | bytes 4194304 | tf_op jit(solution)/shard_map/all_to_all | solution.py:181
  172.5 0.0 collective-permute-start
  172.5 25.7 %collective-permute-done = bf16[128,8192]{0,1:T(8,128)(2,1)S(1)} collective-permute-done((bf16[128,8192]{0,1:T(8,128)(2,1)}, bf16[128,8192]{0,1:T(8,128)(2,1)S(1)}, u32[]{:S(2)}, u32[]{:S(2)}) %collective-permute-start) | collective-permute-done | bytes 2097184 | tf_op jit(solution)/shard_map/ppermute | solution.py:21
  198.2 2.9 %copy.55 = bf16[1,128,8192]{2,1,0:T(8,128)(2,1)} copy(bf16[1,128,8192]{1,2,0:T(8,128)(2,1)S(1)} %bitcast.71) | data formatting | bytes 4194304 | tf_op jit(solution)/shard_map/broadcast_in_dim | solution.py:190
  (4 shorter events, 0.0 us)
Async XLA Ops:
  0.0 16.7 %copy-start = (bf16[1,128,8192]{2,1,0:T(8,128)(2,1)S(1)}, bf16[1,128,8192]{2,1,0:T(8,128)(2,1)}, u32[]{:S(2)}) copy-start(bf16[1,128,8192]{2,1,0:T(8,128)(2,1)} %param.5) | copy-start | bytes 6291460
  1.4 11.9 %all-to-all-start = ((bf16[128,4,1]{0,2,1:T(2,128)(2,1)}), bf16[128,4,1]{0,2,1:T(2,128)(2,1)S(1)}, u32[]{:S(2)}, u32[]{:S(2)}) async-start(bf16[128,4,1]{0,2,1:T(2,128)(2,1)} %broadcast_in_dim.51), calls=%async_computation | async-start | bytes 4096 | tf_op jit(solution)/shard_map/all_to_all | solution.py:170
  9.5 10.2 %copy-start.1 = (bf16[1,128,1024]{2,1,0:T(8,128)(2,1)S(1)}, bf16[1,128,1024]{2,1,0:T(8,128)(2,1)}, u32[]{:S(2)}) copy-start(bf16[1,128,1024]{2,1,0:T(8,128)(2,1)} %param.7) | copy-start | bytes 786436
  13.3 10.5 %all-to-all-start.1 = ((bf16[128,4,256]{0,2,1:T(8,128)(2,1)}), bf16[128,4,256]{0,2,1:T(8,128)(2,1)S(1)}, u32[]{:S(2)}, u32[]{:S(2)}) async-start(bf16[128,4,256]{0,2,1:T(8,128)(2,1)} %bitcast.8), calls=%async_computation.1 | async-start | bytes 524288 | tf_op jit(solution)/shard_map/all_to_all | solution.py:168
  23.8 10.2 %all-to-all-start.3 = ((bf16[128,4,256]{0,2,1:T(8,128)(2,1)}), bf16[128,4,256]{0,2,1:T(8,128)(2,1)S(1)}, u32[]{:S(2)}, u32[]{:S(2)}) async-start(bf16[128,4,256]{0,2,1:T(8,128)(2,1)} %bitcast.17), calls=%async_computation.3 | async-start | bytes 524288 | tf_op jit(solution)/shard_map/all_to_all | solution.py:169
  33.9 48.0 %all-to-all-start.2 = ((bf16[128,4,2048]{0,2,1:T(8,128)(2,1)}), bf16[128,4,2048]{0,2,1:T(8,128)(2,1)S(1)}, u32[]{:S(2)}, u32[]{:S(2)}) async-start(bf16[128,4,2048]{0,2,1:T(8,128)(2,1)} %bitcast.13), calls=%async_computation.2 | async-start | bytes 4194304 | tf_op jit(solution)/shard_map/all_to_all | solution.py:167
  172.5 25.7 %collective-permute-start = (bf16[128,8192]{0,1:T(8,128)(2,1)}, bf16[128,8192]{0,1:T(8,128)(2,1)S(1)}, u32[]{:S(2)}, u32[]{:S(2)}) collective-permute-start(bf16[128,8192]{0,1:T(8,128)(2,1)} %bitcast.70), channel_id=1, source_target_pairs={{12,0},{0,4},{4,8},{8,12},{13,1},{1,5},{5,9},{9,13},{14,2},{2,6},{... | collective-permute-start | bytes 6291464 | tf_op jit(solution)/shard_map/ppermute | solution.py:21
where the time goes:
time: 202 us; the launch traced here: 201 us
  waiting for transfers between devices  77.8 us (39%)
  blocking collectives  51.3 us (25%)
  local copies, waits for them, and re-layouts  30.3 us (15%)
  starting transfers between devices  16.8 us (8%)
  other arithmetic  14.9 us (7%)
  matrix products  9.84 us (5%)
    all_to_all x1, blocking collectives, on_device(): lax.all_to_all(heads_out.reshape(sequence_total, 1, per_device * HEAD_SIZ...  51.3 us
    all_to_all x1, waiting for transfers between devices, on_device(): lax.all_to_all(query_send, 'seq', split_axis=1, concat_axis=0, tiled=True)  43.6 us
    ppermute x1, waiting for transfers between devices, passed_along(): return lax.ppermute(block, axis, route)  25.7 us
    unnamed x10, local copies, waits for them, and re-layouts  16.7 us
    all_to_all x1, starting transfers between devices, on_device(): lax.all_to_all(segment_send, 'seq', split_axis=1, concat_axis=0, tiled=True)  6.35 us
    dot_general x1, matrix products, online_update(): jnp.einsum('qkgn,nkd->qkgd', weights.astype(jnp.bfloat16), value_block, p...  6.04 us
  transfers between devices with their start and end apart: 5, of which 5 were waited for; matrix products, arithmetic and copies ran while one was open for 6% of the time, Pallas kernels for 0%

commit v1 on v0

--- a/solution.py
+++ b/solution.py
@@ -13,6 +13,12 @@
 fast_beta = 32.0
 slow_beta = 1.0
 masked_score = -1e30
+
+
+def swap_blocks(value, mesh_axis, split, join):
+    shards = jnp.split(value, lax.axis_size(mesh_axis), axis=split)
+    received = lax.all_to_all(jnp.stack(shards), mesh_axis, 0, 0)
+    return jnp.concatenate(received, axis=join)
 
 
 def passed_along(block, axis, distance):
@@ -164,7 +170,7 @@
         segment_ids.astype(jnp.bfloat16)[:, None, None], (token_rows, row_width, 1)
     )
     query_all, key_all, value_all, segment_all = (
-        lax.all_to_all(query_send, "seq", split_axis=1, concat_axis=0, tiled=True),
+        swap_blocks(query_send, "seq", 1, 0),
         lax.all_to_all(key_send, "seq", split_axis=1, concat_axis=0, tiled=True),
         lax.all_to_all(value_send, "seq", split_axis=1, concat_axis=0, tiled=True),
         lax.all_to_all(segment_send, "seq", split_axis=1, concat_axis=0, tiled=True),

time: 202 us -> 208 us (1.030)
  waiting for transfers between devices: 77.8 us -> 80.6 us
    all_to_all x1, waiting for transfers between devices: 2.38 us -> 5.2 us  [on_device(): lax.all_to_all(value_send, 'seq', split_axis=1, concat_axis=0, tiled=True)]
    all_to_all x1, waiting for transfers between devices: 2.79 us -> 0.01 us  [on_device(): lax.all_to_all(segment_send, 'seq', split_axis=1, concat_axis=0, tiled=True)]
    another operation x2 -> x3, other arithmetic: 2.92 us -> 4.49 us
    unnamed x10 -> x8, local copies, waits for them, and re-layouts: 16.7 us -> 16.7 us
  transfers between devices with their start and end apart: 5 -> 5, of which waited for: 5 -> 4; matrix products, arithmetic and copies ran while one was open for 6% -> 6% of each run, Pallas kernels for 0% -> 0%
where the time goes in v1:
time: 208 us; the launch traced here: 207 us
  waiting for transfers between devices  80.6 us (39%)
  blocking collectives  51.3 us (25%)
  local copies, waits for them, and re-layouts  31.9 us (15%)
  starting transfers between devices  18.6 us (9%)
  other arithmetic  15 us (7%)
  matrix products  9.85 us (5%)
    all_to_all x1, blocking collectives, on_device(): lax.all_to_all(heads_out.reshape(sequence_total, 1, per_device * HEAD_SIZ...  51.3 us
    all_to_all x1, waiting for transfers between devices, swap_blocks(): received = lax.all_to_all(jnp.stack(shards), mesh_axis, 0, 0)  44.5 us
    ppermute x1, waiting for transfers between devices, passed_along(): return lax.ppermute(block, axis, route)  25.7 us
    unnamed x8, local copies, waits for them, and re-layouts  16.7 us
    all_to_all x1, starting transfers between devices, on_device(): lax.all_to_all(segment_send, 'seq', split_axis=1, concat_axis=0, tiled=True)  6.35 us
    dot_general x1, matrix products, online_update(): jnp.einsum('qkgn,nkd->qkgd', weights.astype(jnp.bfloat16), value_block, p...  6.04 us
    all_to_all x1, waiting for transfers between devices, on_device(): lax.all_to_all(key_send, 'seq', split_axis=1, concat_axis=0, tiled=True)  5.28 us
    all_to_all x1, waiting for transfers between devices, on_device(): lax.all_to_all(value_send, 'seq', split_axis=1, concat_axis=0, tiled=True)  5.2 us
  transfers between devices with their start and end apart: 5, of which 4 were waited for; matrix products, arithmetic and copies ran while one was open for 6% of the time, Pallas kernels for 0%

profile of v1, /device:TPU:0, one launch (start us, length us, event | category | flops | bytes accessed | tf_op | source)
XLA Modules:
  0.0 207.4 jit_solution(5358513350038586653)
XLA Ops:
  0.0 0.7 convert_bitcast_fusion.1
  0.7 0.6 broadcast_in_dim.51
  1.3 6.3 %all-to-all-start = ((bf16[128,4,1]{0,2,1:T(2,128)(2,1)}), bf16[128,4,1]{0,2,1:T(2,128)(2,1)S(1)}, u32[]{:S(2)}, u32[]{:S(2)}) async-start(bf16[128,4,1]{0,2,1:T(2,128)(2,1)} %broadcast_in_dim.51), calls=%async_computation | async-start | bytes 4096 | tf_op jit(solution)/shard_map/all_to_all | solution.py:176
  7.6 0.7 convert_bitcast_fusion
  8.3 0.0 copy-start
  8.3 1.1 copy.53
  9.4 0.2 fusion.15
  9.6 0.1 subtract_convert_fusion.1
  9.7 0.7 pad_maximum_fusion.2
  10.4 4.3 %copy.55 = f32[1,128,8192]{1,2,0:T(8,128)} copy(bf16[1,128,8192]{2,1,0:T(8,128)(2,1)} %param.5) | data formatting | bytes 6291456 | tf_op jit(solution)/shard_map/convert_element_type | solution.py:141
  14.7 0.0 copy-done
  14.7 0.8 copy.61
  15.6 0.0 all-to-all-done
  15.6 5.1 %all-to-all-start.1 = ((bf16[128,4,256]{0,2,1:T(8,128)(2,1)}), bf16[128,4,256]{0,2,1:T(8,128)(2,1)S(1)}, u32[]{:S(2)}, u32[]{:S(2)}) async-start(bf16[128,4,256]{0,2,1:T(8,128)(2,1)} %bitcast.8), calls=%async_computation.1 | async-start | bytes 524288 | tf_op jit(solution)/shard_map/all_to_all | solution.py:174
  20.7 2.8 %subtract_convert_fusion = (bf16[128,64,64]{0,2,1:T(8,128)(2,1)S(1)}, bf16[128,64,64]{0,2,1:T(8,128)(2,1)S(1)}) fusion(f32[128,64,128]{0,2,1:T(8,128)} %bitcast.69, f32[128,64]{0,1:T(8,128)S(1)} %get-tuple-element.114, f32[128,64]{0,1:T(8,128)S(1)} %get-tuple-element.113), kind=kLoop, calls=%fused_computation.15 | loop fusion | flops 4194304 | bytes 6356992 | tf_op jit(solution)/shard_map/convert.5
  23.5 0.2 pad_maximum_fusion
  23.7 5.3 %all-to-all-done.1 = bf16[128,4,256]{0,2,1:T(8,128)(2,1)S(1)} async-done(((bf16[128,4,256]{0,2,1:T(8,128)(2,1)}), bf16[128,4,256]{0,2,1:T(8,128)(2,1)S(1)}, u32[]{:S(2)}, u32[]{:S(2)}) %all-to-all-start.1) | async-done | bytes 262176 | tf_op jit(solution)/shard_map/all_to_all | solution.py:174
  29.0 3.4 %all-to-all-start.3 = ((bf16[128,4,256]{0,2,1:T(8,128)(2,1)}), bf16[128,4,256]{0,2,1:T(8,128)(2,1)S(1)}, u32[]{:S(2)}, u32[]{:S(2)}) async-start(bf16[128,4,256]{0,2,1:T(8,128)(2,1)} %bitcast.19), calls=%async_computation.3 | async-start | bytes 524288 | tf_op jit(solution)/shard_map/all_to_all | solution.py:175
  32.4 0.1 slice_bitcast_fusion.3
  32.5 1.6 pad_maximum_fusion.1
  34.1 5.2 %all-to-all-done.3 = bf16[128,4,256]{0,2,1:T(8,128)(2,1)S(1)} async-done(((bf16[128,4,256]{0,2,1:T(8,128)(2,1)}), bf16[128,4,256]{0,2,1:T(8,128)(2,1)S(1)}, u32[]{:S(2)}, u32[]{:S(2)}) %all-to-all-start.3) | async-done | bytes 262176 | tf_op jit(solution)/shard_map/all_to_all | solution.py:175
  39.3 3.8 %all-to-all-start.2 = ((bf16[4,128,1,2048]{1,3,2,0:T(8,128)(2,1)}), bf16[4,128,1,2048]{1,3,2,0:T(8,128)(2,1)S(1)}, u32[]{:S(2)}, u32[]{:S(2)}) async-start(bf16[4,128,1,2048]{1,3,2,0:T(8,128)(2,1)} %pad_maximum_fusion.1), calls=%async_computation.2 | async-start | bytes 4194304 | tf_op jit(solution)/shard_map/all_to_all | solution.py:20
  43.1 0.2 fusion.12
  43.3 0.1 copy.54
  43.5 0.1 reshape.179
  43.6 0.2 copy.62
  43.8 0.1 reshape.187
  43.9 44.5 %all-to-all-done.2 = bf16[4,128,1,2048]{1,3,2,0:T(8,128)(2,1)S(1)} async-done(((bf16[4,128,1,2048]{1,3,2,0:T(8,128)(2,1)}), bf16[4,128,1,2048]{1,3,2,0:T(8,128)(2,1)S(1)}, u32[]{:S(2)}, u32[]{:S(2)}) %all-to-all-start.2) | async-done | bytes 2097184 | tf_op jit(solution)/shard_map/all_to_all | solution.py:20
  88.4 2.6 %copy.58 = bf16[4,128,1,2048]{3,1,0,2:T(8,128)(2,1)} copy(bf16[4,128,1,2048]{1,3,2,0:T(8,128)(2,1)S(1)} %all-to-all-done.2) | data formatting | bytes 4194304 | tf_op jit(solution)/shard_map/all_to_all | solution.py:20
  90.9 2.2 %copy.74 = bf16[64,8,16,128]{3,2,1,0:T(8,128)(2,1)S(1)} copy(bf16[64,8,16,128]{3,1,2,0:T(8,128)(2,1)} %bitcast.73) | data formatting | bytes 4194304
  93.2 3.8 %fusion = (f32[512,2,8]{0,2,1:T(8,128)S(1)}, f32[2,512,512,8]{2,1,3,0:T(8,128)S(1)}) fusion(pred[512,512]{0,1:T(8,128)(4,1)S(1)} %fusion.12, bf16[512,2,8,128]{3,2,1,0:T(8,128)(2,1)S(1)} %bitcast.70, bf16[512,2,128,1]{2,1,0,3:T(2,128)(2,1)S(1)} %bitcast.78), kind=kOutput, calls=%fused_computation.2 | convolution fusion | flops 1086316544 | bytes 19431424 | tf_op jit(solution)/shard_map/while/body/eval_jaxpr/while/body/qkgd,nkd->qkgn/dot_general | solution.py:78
  97.0 4.0 %fusion.1 = f32[512,2,8]{0,2,1:T(8,128)S(1)} fusion(f32[2,512,512,8]{2,1,3,0:T(8,128)S(1)} %get-tuple-element.116, f32[512,2,8]{0,2,1:T(8,128)S(1)} %broadcast_maximum_fusion, pred[512,512]{0,1:T(8,128)(4,1)S(1)} %fusion.12), kind=kLoop, calls=%fused_computation.3 | loop fusion | flops 20963328 | bytes 17104896 | tf_op jit(solution)/shard_map/while/body/eval_jaxpr/while/body/reduce_sum | solution.py:86
  101.0 6.0 %fusion.7 = bf16[512,2,8,128]{0,3,2,1:T(8,128)(2,1)} fusion(f32[2,512,512,8]{2,1,3,0:T(8,128)S(1)} %get-tuple-element.116, f32[512,2,8]{0,2,1:T(8,128)S(1)} %broadcast_maximum_fusion, pred[512,512]{0,1:T(8,128)(4,1)S(1)} %fusion.12, f32[512,2,8]{0,2,1:T(8,128)S(1)} %get-tuple-element.112, f32[512,2,8]{0,2,1:T(8,128)S(1)} %get-tuple-element.111, ...), kind=kOutput, calls=%fused_computation.9 | convolution fusion | flops 1097859072 | bytes 19496960 | tf_op jit(solution)/shard_map/while/body/eval_jaxpr/while/body/qkgn,nkd->qkgd/dot_general | solution.py:87
  107.1 0.5 broadcast.185
  107.6 3.8 %reduce = bf16[512,2048]{0,1:T(8,128)(2,1)S(1)} reduce(bf16[512,1,2048]{0,2,1:T(8,128)(2,1)} %bitcast.74, bf16[]{:T(256)} %broadcast.185), dimensions={1}, to_apply=%copy.64.reduce_sub_computation | reduce | bytes 4194306 | tf_op jit(solution)/shard_map/while/body/eval_jaxpr/convert_element_type | solution.py:99
  111.4 2.4 %copy.83 = bf16[512,2048]{1,0:T(8,128)(2,1)} copy(bf16[512,2048]{0,1:T(8,128)(2,1)S(1)} %reduce) | data formatting | bytes 4194304
  113.8 4.5 %reshape.189 = bf16[4,2,131072]{2,1,0:T(2,128)(2,1)} reshape(bf16[512,2048]{1,0:T(8,128)(2,1)} %copy.83) | data formatting | bytes 4194304
  118.2 51.3 %all_to_all.59 = bf16[4,2,131072]{2,1,0:T(2,128)(2,1)S(1)} all-to-all(bf16[4,2,131072]{2,1,0:T(2,128)(2,1)} %reshape.189), channel_id=1, replica_groups=mesh['dp'=2,'pipe'=4,'seq'=4] {'seq'}, dimensions={0} | all-to-all | bytes 4194304 | tf_op jit(solution)/shard_map/all_to_all | solution.py:187
  169.6 3.4 %reshape.190 = bf16[512,1,2048]{2,1,0:T(2,128)(2,1)} reshape(bf16[4,2,131072]{2,1,0:T(2,128)(2,1)S(1)} %all_to_all.59) | data formatting | bytes 4194304
  172.9 3.5 %copy.73 = bf16[512,1,2048]{2,0,1:T(8,128)(2,1)S(1)} copy(bf16[512,1,2048]{2,1,0:T(2,128)(2,1)} %reshape.190) | data formatting | bytes 4194304
  176.4 2.5 %copy.65 = bf16[128,4,1,2048]{0,3,1,2:T(8,128)(2,1)} copy(bf16[128,4,1,2048]{3,0,1,2:T(8,128)(2,1)S(1)} %bitcast.71) | data formatting | bytes 4194304 | tf_op jit(solution)/shard_map/all_to_all | solution.py:187
  178.9 0.0 collective-permute-start
  178.9 25.7 %collective-permute-done = bf16[128,8192]{0,1:T(8,128)(2,1)S(1)} collective-permute-done((bf16[128,8192]{0,1:T(8,128)(2,1)}, bf16[128,8192]{0,1:T(8,128)(2,1)S(1)}, u32[]{:S(2)}, u32[]{:S(2)}) %collective-permute-start) | collective-permute-done | bytes 2097184 | tf_op jit(solution)/shard_map/ppermute | solution.py:27
  204.5 2.9 %copy.66 = bf16[1,128,8192]{2,1,0:T(8,128)(2,1)} copy(bf16[1,128,8192]{1,2,0:T(8,128)(2,1)S(1)} %bitcast.76) | data formatting | bytes 4194304 | tf_op jit(solution)/shard_map/broadcast_in_dim | solution.py:196
  (4 shorter events, 0.0 us)
Async XLA Ops:
  1.3 14.3 %all-to-all-start = ((bf16[128,4,1]{0,2,1:T(2,128)(2,1)}), bf16[128,4,1]{0,2,1:T(2,128)(2,1)S(1)}, u32[]{:S(2)}, u32[]{:S(2)}) async-start(bf16[128,4,1]{0,2,1:T(2,128)(2,1)} %broadcast_in_dim.51), calls=%async_computation | async-start | bytes 4096 | tf_op jit(solution)/shard_map/all_to_all | solution.py:176
  8.3 6.4 %copy-start = (bf16[1,128,1024]{2,1,0:T(8,128)(2,1)S(1)}, bf16[1,128,1024]{2,1,0:T(8,128)(2,1)}, u32[]{:S(2)}) copy-start(bf16[1,128,1024]{2,1,0:T(8,128)(2,1)} %param.7) | copy-start | bytes 786436
  15.6 13.4 %all-to-all-start.1 = ((bf16[128,4,256]{0,2,1:T(8,128)(2,1)}), bf16[128,4,256]{0,2,1:T(8,128)(2,1)S(1)}, u32[]{:S(2)}, u32[]{:S(2)}) async-start(bf16[128,4,256]{0,2,1:T(8,128)(2,1)} %bitcast.8), calls=%async_computation.1 | async-start | bytes 524288 | tf_op jit(solution)/shard_map/all_to_all | solution.py:174
  29.0 10.3 %all-to-all-start.3 = ((bf16[128,4,256]{0,2,1:T(8,128)(2,1)}), bf16[128,4,256]{0,2,1:T(8,128)(2,1)S(1)}, u32[]{:S(2)}, u32[]{:S(2)}) async-start(bf16[128,4,256]{0,2,1:T(8,128)(2,1)} %bitcast.19), calls=%async_computation.3 | async-start | bytes 524288 | tf_op jit(solution)/shard_map/all_to_all | solution.py:175
  39.3 49.1 %all-to-all-start.2 = ((bf16[4,128,1,2048]{1,3,2,0:T(8,128)(2,1)}), bf16[4,128,1,2048]{1,3,2,0:T(8,128)(2,1)S(1)}, u32[]{:S(2)}, u32[]{:S(2)}) async-start(bf16[4,128,1,2048]{1,3,2,0:T(8,128)(2,1)} %pad_maximum_fusion.1), calls=%async_computation.2 | async-start | bytes 4194304 | tf_op jit(solution)/shard_map/all_to_all | solution.py:20
  178.9 25.7 %collective-permute-start = (bf16[128,8192]{0,1:T(8,128)(2,1)}, bf16[128,8192]{0,1:T(8,128)(2,1)S(1)}, u32[]{:S(2)}, u32[]{:S(2)}) collective-permute-start(bf16[128,8192]{0,1:T(8,128)(2,1)} %bitcast.75), channel_id=1, source_target_pairs={{12,0},{0,4},{4,8},{8,12},{13,1},{1,5},{5,9},{9,13},{14,2},{2,6},{... | collective-permute-start | bytes 6291464 | tf_op jit(solution)/shard_map/ppermute | solution.py:27
